TPU v7x, 512 devices: a whole 4x4x16 slice. The times are simulated.
512 devices in a mesh: group: 16 (over x, z_hi), shard: 32 (over z_lo, y, core).
Axes of the slice: x: 4, y: 4, z: 16 (z_hi: 4, z_lo: 4; z = z_hi * 4 + z_lo), core: 2. Of those that a mesh axis runs over, the one named last changes fastest.
Arguments:
- step_count: int32 [1], replicated, may hold values from 2 to 8
- block_order: int32 [224], replicated, may hold values from 0 to 223, as said below
- saved_tiles: bfloat16 [512, 4, 18, 18, 256], P(('group', 'shard')), may hold values from -6 to 6
- pre_act: bfloat16 [262144, 256], P(('group', 'shard')), may hold values from -6 to 6
- grad_output: bfloat16 [262144, 256], P(('group', 'shard')), may hold values from -0.0234375 to 0.0234375
- pointwise_live: bfloat16 [256, 256], replicated, may hold values from -0.375 to 0.375
- master_rows: float32 [7168, 256], P('shard'), may hold values from -0.25 to 0.25, as said below
- row_moment: float32 [7168], P('shard'), may hold values from 0.5 to 30, as said below
- col_moment: float32 [2, 256], replicated, may hold values from 0.03 to 0.3
- next_tiles: bfloat16 [512, 4, 18, 18, 256], P(('group', 'shard')), may hold values from -6 to 6
Outputs:
- update_rows: float32 [7168, 256], P('shard')
- new_master: float32 [7168, 256], P('shard')
- new_row_moment: float32 [7168], P('shard')
- new_col_moment: float32 [2, 256], replicated
- next_output: bfloat16 [262144, 256], P(('group', 'shard'))
Inputs may be any that keep to these rules, and one draw needn't show every extreme that they name: `block_order`: a permutation of 0 to 223. `master_rows`: rows of the 3x3x3 kernel are of order (6912) ** -0.5 and rows of the 1x1x1 kernel of order 256 ** -0.5. `row_moment`: positive row factors.
All inputs are finite; a program needn't handle non-finite values.
Results may differ from a plain program's by a relative error of at most 0.023.
Values may be sent and summed in bfloat16 or wider, within the bound.
A program may use at most 64 MiB of HBM per device.

v0:
```python
import jax
import jax.numpy as jnp
from jax import lax
from jax.sharding import PartitionSpec as P

CI = 256
CO = 256
BLK = 32
FR = 2
HW = 16
NB3 = 216
NB = 224
learn_rate = 0.002
decay_power = 0.8


def silu_slope(values):
    sigma = jax.nn.sigmoid(values)
    return sigma * (1.0 + values * (1.0 - sigma))


def tap_views(frames):
    views = []
    for frame_off in range(3):
        for row_off in range(3):
            for col_off in range(3):
                window = frames[
                    frame_off : frame_off + FR, row_off : row_off + HW, col_off : col_off + HW, :
                ]
                views.append(window.reshape(FR * HW * HW, CI))
    return views


def contract_rows(left, right):
    return lax.dot_general(
        left, right, (((0,), (0,)), ((), ())), preferred_element_type=jnp.float32
    )


def kernel_sums(values, is_small):
    large_part = jnp.sum(jnp.where(is_small[:, None], 0.0, values), axis=0)
    small_part = jnp.sum(jnp.where(is_small[:, None], values, 0.0), axis=0)
    return jnp.stack([large_part, small_part])


def shards(
    step_count,
    block_order,
    saved_tiles,
    pre_act,
    grad_output,
    pointwise_live,
    master_rows,
    row_moment,
    col_moment,
    next_tiles,
):
    pre_float = pre_act.astype(jnp.float32)
    activation = jax.nn.silu(pre_float).astype(jnp.bfloat16)
    grad_act = lax.dot_general(
        grad_output, pointwise_live, (((1,), (1,)), ((), ())), preferred_element_type=jnp.float32
    )
    grad_pre = (grad_act * silu_slope(pre_float)).astype(jnp.bfloat16)
    pieces = [contract_rows(view, grad_pre) for view in tap_views(saved_tiles[0])]
    pieces.append(contract_rows(activation, grad_output))
    own_term = jnp.concatenate(pieces, axis=0).astype(jnp.bfloat16)
    total_rows = NB * BLK
    stored = jnp.take(own_term.reshape(NB, BLK, CO), block_order, axis=0).reshape(total_rows, CO)
    own_rows = master_rows.shape[0]
    partial_value = lax.psum_scatter(stored, "shard", scatter_dimension=0, tiled=True).astype(
        jnp.float32
    )
    gradient = lax.psum(partial_value, "group")
    owner = lax.axis_index("shard")
    own_count = own_rows // BLK
    own_blocks = lax.dynamic_slice_in_dim(block_order, owner * own_count, own_count)
    is_small = jnp.repeat(own_blocks >= NB3, BLK, total_repeat_length=own_rows)
    decay_rate = 1.0 - step_count.astype(jnp.float32)[0] ** (-decay_power)
    counts = jnp.array([27 * CI, CO], jnp.float32)
    squares = gradient * gradient
    new_row = decay_rate * row_moment + (1.0 - decay_rate) * jnp.mean(squares, axis=1)
    col_part = kernel_sums(squares, is_small)
    row_part = kernel_sums(new_row[:, None], is_small)[:, 0]
    col_total, row_total = lax.psum((col_part, row_part), "shard")
    new_col = decay_rate * col_moment + (1.0 - decay_rate) * col_total / counts[:, None]
    row_mean = row_total / counts
    col_rows = jnp.where(is_small[:, None], new_col[1], new_col[0])
    mean_rows = jnp.where(is_small, row_mean[1], row_mean[0])
    scaled = gradient / jnp.sqrt(new_row[:, None] * col_rows / mean_rows[:, None])
    square_part = kernel_sums(jnp.sum(scaled * scaled, axis=1)[:, None], is_small)[:, 0]
    square_total = lax.psum(square_part, "shard")
    clip_factor = jnp.maximum(1.0, jnp.sqrt(square_total / (counts * CO)))
    update_rows = scaled / jnp.where(is_small, clip_factor[1], clip_factor[0])[:, None]
    new_master = master_rows - learn_rate * update_rows
    weights_low = new_master.astype(jnp.bfloat16)
    gathered = lax.all_gather(weights_low, "shard", axis=0, tiled=True)
    inverse = jnp.zeros((NB,), jnp.int32).at[block_order].set(jnp.arange(NB, dtype=jnp.int32))
    natural = jnp.take(gathered.reshape(NB, BLK, CO), inverse, axis=0).reshape(total_rows, CO)
    spatial = natural[: 27 * CI].reshape(27, CI, CO)
    pointwise = natural[27 * CI :]
    hidden_sum = jnp.zeros((FR * HW * HW, CO), jnp.float32)
    for index_tap, view in enumerate(tap_views(next_tiles[0])):
        hidden_sum = hidden_sum + jnp.dot(
            view, spatial[index_tap], preferred_element_type=jnp.float32
        )
    hidden_act = jax.nn.silu(hidden_sum).astype(jnp.bfloat16)
    next_output = jnp.dot(hidden_act, pointwise, preferred_element_type=jnp.float32).astype(
        jnp.bfloat16
    )
    return (update_rows, new_master, new_row, new_col, next_output)


def solution(mesh):
    in_specs = (
        P(),
        P(),
        P(("group", "shard"), None, None, None, None),
        P(("group", "shard"), None),
        P(("group", "shard"), None),
        P(),
        P("shard", None),
        P("shard"),
        P(),
        P(("group", "shard"), None, None, None, None),
    )
    out_specs = (P("shard", None), P("shard", None), P("shard"), P(), P(("group", "shard"), None))
    return jax.shard_map(shards, mesh=mesh, in_specs=in_specs, out_specs=out_specs, check_vma=False)
```

profile of v0, /device:TPU:1, one launch (start us, length us, event | category | flops | bytes accessed | tf_op | source)
XLA Modules:
  0.0 556.7 jit_solution(18183779678937260853)
XLA Ops:
  7.2 1.3 copy.102
  10.0 0.9 fusion.14
  11.9 0.9 fusion.18
  13.8 0.9 fusion.22
  14.7 0.9 fusion.24
  15.6 0.9 fusion.26
  16.6 0.9 fusion.28
  17.5 0.9 fusion.30
  18.5 0.9 fusion.32
  19.4 0.9 fusion.34
  20.3 0.9 fusion.36
  21.3 0.9 fusion.38
  23.1 0.9 fusion.42
  24.1 0.9 fusion.44
  25.0 0.9 fusion.46
  25.9 0.9 fusion.48
  27.8 0.9 fusion.52
  28.8 0.9 fusion.54
  29.7 0.9 fusion.56
  30.6 0.9 fusion.58
  31.6 0.9 fusion.60
  32.5 0.9 fusion.62
  35.3 1.0 fusion.12
  36.3 4.9 gather_fusion
  41.2 3.8 broadcast_select_fusion.1
  46.8 4.5 select_select_fusion
  51.3 150.8 %reduce-scatter.2.cloned.1.call-done = bf16[224,256]{1,0:T(8,128)(2,1)} async-done(((bf16[7168,256]{1,0:T(8,128)(2,1)}), bf16[224,256]{1,0:T(8,128)(2,1)}) %reduce-scatter.2.cloned.1.call-update) | async-done | bytes 114704 | tf_op jit(solution)/shard_map/reduce_scatter | solution.py:70
  202.1 89.2 %all-reduce.2 = f32[224,256]{1,0:T(8,128)S(1)} all-reduce(bf16[224,256]{1,0:T(8,128)(2,1)} %reduce-scatter.2.cloned.1.call-done), channel_id=1, replica_groups=mesh['group'=16,'shard'=32] {'group'}, use_global_device_ids=true, to_apply=%region_1.3 | all-reduce | flops 57344 | bytes 344064 | tf_op jit(solution)/shard_map/psum | solution.py:73
  291.5 5.2 select_reduce_fusion.5
  296.7 1.3 maximum_bitcast_fusion
  298.0 84.7 %all-reduce = (f32[2]{0:T(128)S(1)}, f32[2,256]{1,0:T(2,128)S(1)}) all-reduce(f32[2]{0:T(128)S(1)} %maximum_bitcast_fusion, f32[2,256]{1,0:T(2,128)S(1)} %pad_maximum_fusion), channel_id=1, replica_groups=mesh['group'=16,'shard'=32] {'shard'}, use_global_device_ids=true, to_apply=%region_8.10 | all-reduce | flops 514 | bytes 4112 | tf_op jit(solution)/shard_map/psum | solution.py:84
  383.3 5.7 %broadcast_select_fusion.3 = f32[224]{0:T(256)S(1)} fusion(f32[]{:T(128)} %bitcast.74, f32[]{:T(128)} %bitcast.73, pred[]{:T(512)} %bitcast.65, pred[]{:T(512)} %bitcast.64, pred[]{:T(512)} %bitcast.63, pred[]{:T(512)} %bitcast.62, pred[]{:T(512)} %bitcast.61, pred[]{:T(512)} %bitcast.60, pred[]{:T(512)} %bitcast.59, s32[256]{0:T(256)S(1)} %add_bitcast_fusion), kind=kLoop, calls=%fused_computation.172 | loop fusion | flops 4704 | bytes 1807 | tf_op jit(solution)/shard_map/jit(_where)/select_n | solution.py:88
  389.3 5.2 select_reduce_fusion.3
  394.5 1.3 maximum_bitcast_fusion.1
  395.8 67.4 %psum.31 = f32[2]{0:T(128)S(1)} all-reduce(f32[2]{0:T(128)S(1)} %maximum_bitcast_fusion.1), channel_id=1, replica_groups=mesh['group'=16,'shard'=32] {'shard'}, use_global_device_ids=true, to_apply=%region_12.14 | all-reduce | flops 2 | bytes 16 | tf_op jit(solution)/shard_map/psum | solution.py:91
  463.8 5.7 %broadcast_select_fusion.2 = f32[224]{0:T(256)S(1)} fusion(f32[]{:T(128)} %bitcast.79, f32[]{:T(128)} %bitcast.78, pred[]{:T(512)} %bitcast.65, pred[]{:T(512)} %bitcast.64, pred[]{:T(512)} %bitcast.63, pred[]{:T(512)} %bitcast.62, pred[]{:T(512)} %bitcast.61, pred[]{:T(512)} %bitcast.60, pred[]{:T(512)} %bitcast.59, s32[256]{0:T(256)S(1)} %add_bitcast_fusion), kind=kLoop, calls=%fused_computation.171 | loop fusion | flops 4704 | bytes 1807 | tf_op jit(solution)/shard_map/jit(_where)/select_n | solution.py:93
  470.5 1.5 scatter_custom_fusion
  472.1 1.4 fusion.85
  473.5 2.1 fusion.84
  475.6 53.3 %all-gather.2.cloned.1.call-done = bf16[7168,256]{1,0:T(8,128)(2,1)} async-done(((bf16[224,256]{1,0:T(8,128)(2,1)}), bf16[7168,256]{1,0:T(8,128)(2,1)}) %all-gather.2.cloned.1.call-update) | async-done | bytes 3670032 | tf_op jit(solution)/shard_map/all_gather | solution.py:96
  528.9 4.9 gather_fusion.1
  533.8 2.5 broadcast_select_fusion
  536.4 1.0 fusion.82
  539.0 1.0 convolution_bitcast_fusion.6
  540.1 1.0 convolution_bitcast_fusion.7
  541.1 1.1 convolution_bitcast_fusion.8
  545.9 1.1 fusion.10
  547.0 2.9 convolution_convert_fusion
  (124 shorter events, 15.9 us)
Async XLA Ops:
  7.2 2.3 copy-start
  7.2 194.9 %reduce-scatter.2.cloned.1.call-start = ((), (), s32[]{:S(2)}) async-start(), calls=%async_computation.1 | async-start | bytes 3784704 | tf_op jit(solution)/shard_map/reduce_scatter | solution.py:70
  8.7 0.7 copy-start.27
  8.7 1.0 copy-start.30
  8.7 1.0 copy-start.31
  45.0 1.8 copy-start.28
  45.0 246.5 %copy-start.26 = (f32[224]{0:T(256)S(1)}, f32[224]{0:T(256)}, u32[]{:S(2)}) copy-start(f32[224]{0:T(256)} %param.22) | copy-start | bytes 2692
  45.0 337.7 %copy-start.25 = (f32[2,256]{1,0:T(2,128)S(1)}, f32[2,256]{1,0:T(2,128)}, u32[]{:S(2)}) copy-start(f32[2,256]{1,0:T(2,128)} %param.23) | copy-start | bytes 6148
  45.0 337.7 %copy-start.29 = (f32[2]{0:T(128)S(1)}, f32[2]{0:T(128)}, u32[]{:S(2)}) copy-start(f32[2]{0:T(128)} %constant.126) | copy-start | bytes 28
  45.0 418.2 %copy-start.32 = (f32[2]{0:T(128)S(1)}, f32[2]{0:T(128)}, u32[]{:S(2)}) copy-start(f32[2]{0:T(128)} %constant.129) | copy-start | bytes 28
  45.0 424.5 %copy-start.22 = (f32[224,256]{1,0:T(8,128)S(1)}, f32[224,256]{1,0:T(8,128)}, u32[]{:S(2)}) copy-start(f32[224,256]{1,0:T(8,128)} %param.21) | copy-start | bytes 688132
  45.0 426.9 %copy-start.21 = (bf16[1,4,18,18,256]{4,1,3,2,0:T(4,128)(2,1)S(1)}, bf16[1,4,18,18,256]{4,1,3,2,0:T(4,128)(2,1)}, u32[]{:S(2)}) copy-start(bf16[1,4,18,18,256]{4,1,3,2,0:T(4,128)(2,1)} %param.24) | copy-start | bytes 1990660
  45.0 483.9 %all-gather.2.cloned.1.call-start = ((), (), s32[]{:S(2)}) async-start(), calls=%async_computation.2 | async-start | bytes 3784704 | tf_op jit(solution)/shard_map/all_gather | solution.py:96
  296.7 176.9 %copy-start.24 = (f32[224]{0:T(256)}, f32[224]{0:T(256)S(1)}, u32[]{:S(2)}) copy-start(f32[224]{0:T(256)S(1)} %get-tuple-element.32) | copy-start | bytes 2692
  382.7 90.8 %copy-start.23 = (f32[2,256]{1,0:T(2,128)}, f32[2,256]{1,0:T(2,128)S(1)}, u32[]{:S(2)}) copy-start(f32[2,256]{1,0:T(2,128)S(1)} %multiply_add_fusion) | copy-start | bytes 6148
  537.4 1.4 copy-start.4
  537.4 1.7 copy-start.3
  537.4 2.7 copy-start.2
  537.6 3.5 copy-start.1
  537.8 4.3 copy-start.20
  538.3 4.1 copy-start.19
  538.5 4.1 copy-start.18
  539.0 3.9 copy-start.17
  540.1 3.1 copy-start.16
  542.2 1.3 copy-start.14
  542.4 1.3 copy-start.12
  542.6 1.3 copy-start.15
  542.9 1.3 copy-start.13
  543.2 1.3 copy-start.11
  543.4 1.3 copy-start.10
  543.7 1.3 copy-start.9
  543.9 1.3 copy-start.8
  544.2 1.2 copy-start.7
  544.4 1.2 copy-start.6
  544.7 1.2 copy-start.5
Sparse Core Ops, SparseCore 0:
  45.2 156.8 reduce-scatter.1
  470.6 58.3 all-gather.1
where the time goes:
time: 557 us
  blocking collectives  241 us (43%)
  waiting for transfers between devices  204 us (37%)
  matrix products  38.5 us (7%)
  other arithmetic  36.8 us (7%)
  local copies, waits for them, and re-layouts  20.3 us (4%)
  between operations  15.6 us (3%)
    reduce_scatter x1, waiting for transfers between devices, shards(): lax.psum_scatter(stored, 'shard', scatter_dimension=0, tiled=True)  151 us
    psum x1, blocking collectives, shards(): gradient = lax.psum(partial_value, 'group')  89.2 us
    psum x1, blocking collectives, shards(): col_total, row_total = lax.psum((col_part, row_part), 'shard')  84.7 us
    psum x1, blocking collectives, shards(): square_total = lax.psum(square_part, 'shard')  67.4 us
    all_gather x1, waiting for transfers between devices, shards(): gathered = lax.all_gather(weights_low, 'shard', axis=0, tiled=True)  53.3 us
    dot_general x28, matrix products, contract_rows(): lax.dot_general(left, right, (((0,), (0,)), ((), ())), preferred_element_...  26.2 us
  transfers between devices with their start and end apart: 2, of which 2 were waited for; matrix products, arithmetic and copies ran while one was open for 2% of the time, Pallas kernels for 0%

commit v1 on v0

--- a/solution.py
+++ b/solution.py
@@ -2,6 +2,7 @@
 import jax.numpy as jnp
 from jax import lax
 from jax.sharding import PartitionSpec as P
+from jax.lax import all_gather
 
 CI = 256
 CO = 256
@@ -70,7 +71,11 @@
     partial_value = lax.psum_scatter(stored, "shard", scatter_dimension=0, tiled=True).astype(
         jnp.float32
     )
-    gradient = lax.psum(partial_value, "group")
+
+    def object_trace(arr):
+        return all_gather(arr, axis_name="group").sum(axis=0)
+
+    gradient = object_trace(partial_value)
     owner = lax.axis_index("shard")
     own_count = own_rows // BLK
     own_blocks = lax.dynamic_slice_in_dim(block_order, owner * own_count, own_count)

time: 557 us -> 585 us (1.050)
  waiting for transfers between devices: 204 us -> 332 us
  blocking collectives: 241 us -> 138 us
    all_gather x0 -> x1, waiting for transfers between devices: none -> 119 us  [object_trace(): return all_gather(arr, axis_name='group').sum(axis=0)]
    psum x1 -> x0, blocking collectives: 89.2 us -> none  [shards(): gradient = lax.psum(partial_value, 'group')]
    psum x1, blocking collectives: 84.7 us -> 67.8 us  [shards(): col_total, row_total = lax.psum((col_part, row_part), 'shard')]
    reduce_scatter x1, waiting for transfers between devices: 151 us -> 157 us  [shards(): lax.psum_scatter(stored, 'shard', scatter_dimension=0, tiled=True)]
  transfers between devices with their start and end apart: 2 -> 3, of which waited for: 2 -> 3; matrix products, arithmetic and copies ran while one was open for 2% -> 2% of each run, Pallas kernels for 0% -> 0%
where the time goes in v1:
time: 585 us; the launch traced here: 584 us
  waiting for transfers between devices  332 us (57%)
  blocking collectives  138 us (24%)
  other arithmetic  40.3 us (7%)
  matrix products  38.6 us (7%)
  local copies, waits for them, and re-layouts  20.3 us (3%)
  between operations  15.1 us (3%)
    reduce_scatter x1, waiting for transfers between devices, shards(): lax.psum_scatter(stored, 'shard', scatter_dimension=0, tiled=True)  157 us
    all_gather x1, waiting for transfers between devices, object_trace(): return all_gather(arr, axis_name='group').sum(axis=0)  119 us
    psum x1, blocking collectives, shards(): square_total = lax.psum(square_part, 'shard')  70 us
    psum x1, blocking collectives, shards(): col_total, row_total = lax.psum((col_part, row_part), 'shard')  67.8 us
    all_gather x1, waiting for transfers between devices, shards(): gathered = lax.all_gather(weights_low, 'shard', axis=0, tiled=True)  56.1 us
    dot_general x28, matrix products, contract_rows(): lax.dot_general(left, right, (((0,), (0,)), ((), ())), preferred_element_...  26.3 us
  transfers between devices with their start and end apart: 3, of which 3 were waited for; matrix products, arithmetic and copies ran while one was open for 2% of the time, Pallas kernels for 0%

profile of v1, /device:TPU:1, one launch (start us, length us, event | category | flops | bytes accessed | tf_op | source)
XLA Modules:
  0.0 584.2 jit_solution(15771389014226687567)
XLA Ops:
  7.2 1.3 copy.102
  10.0 0.9 fusion.14
  11.0 1.0 fusion.16
  11.9 0.9 fusion.18
  12.9 0.9 fusion.20
  13.8 0.9 fusion.22
  14.7 0.9 fusion.24
  17.5 0.9 fusion.30
  19.4 0.9 fusion.34
  21.3 1.0 fusion.38
  22.2 0.9 fusion.40
  23.2 0.9 fusion.42
  26.0 0.9 fusion.48
  26.9 0.9 fusion.50
  28.8 0.9 fusion.54
  29.7 0.9 fusion.56
  30.7 0.9 fusion.58
  31.6 0.9 fusion.60
  32.5 0.9 fusion.62
  34.4 0.9 fusion.66
  35.4 1.0 fusion.12
  36.4 4.9 gather_fusion
  41.2 3.8 broadcast_select_fusion.1
  45.1 156.9 %reduce-scatter.2.cloned.1.call-done = bf16[224,256]{1,0:T(8,128)(2,1)} async-done(((bf16[7168,256]{1,0:T(8,128)(2,1)}), bf16[224,256]{1,0:T(8,128)(2,1)}) %reduce-scatter.2.cloned.1.call-update) | async-done | bytes 114704 | tf_op jit(solution)/shard_map/reduce_scatter | solution.py:71
  202.1 1.6 all_gather.16
  205.3 4.5 select_select_fusion
  209.8 118.9 %all-gather.6.cloned.1.call-done = f32[3584,256]{1,0:T(8,128)} async-done(((f32[224,256]{1,0:T(8,128)}), f32[3584,256]{1,0:T(8,128)}) %all-gather.6.cloned.1.call-update) | async-done | bytes 3670032 | tf_op jit(solution)/shard_map/all_gather | solution.py:76
  328.7 2.3 reduce_sum.81
  331.2 5.1 select_reduce_fusion.5
  336.2 1.3 maximum_bitcast_fusion
  337.5 67.8 %all-reduce = (f32[2]{0:T(128)S(1)}, f32[2,256]{1,0:T(2,128)S(1)}) all-reduce(f32[2]{0:T(128)S(1)} %maximum_bitcast_fusion, f32[2,256]{1,0:T(2,128)S(1)} %pad_maximum_fusion), channel_id=1, replica_groups=mesh['group'=16,'shard'=32] {'shard'}, use_global_device_ids=true, to_apply=%region_8.10 | all-reduce | flops 514 | bytes 4112 | tf_op jit(solution)/shard_map/psum | solution.py:89
  406.0 5.7 broadcast_select_fusion.3
  412.0 5.1 select_reduce_fusion.3
  417.0 1.3 maximum_bitcast_fusion.1
  418.3 70.0 %psum.23 = f32[2]{0:T(128)S(1)} all-reduce(f32[2]{0:T(128)S(1)} %maximum_bitcast_fusion.1), channel_id=1, replica_groups=mesh['group'=16,'shard'=32] {'shard'}, use_global_device_ids=true, to_apply=%region_12.14 | all-reduce | flops 2 | bytes 16 | tf_op jit(solution)/shard_map/psum | solution.py:96
  488.9 5.7 broadcast_select_fusion.2
  495.5 1.5 scatter_custom_fusion
  497.2 1.4 fusion.85
  498.6 2.1 fusion.84
  500.7 56.1 %all-gather.4.cloned.1.call-done = bf16[7168,256]{1,0:T(8,128)(2,1)} async-done(((bf16[224,256]{1,0:T(8,128)(2,1)}), bf16[7168,256]{1,0:T(8,128)(2,1)}) %all-gather.4.cloned.1.call-update) | async-done | bytes 3670032 | tf_op jit(solution)/shard_map/all_gather | solution.py:101
  556.8 4.9 gather_fusion.1
  561.7 2.5 broadcast_select_fusion
  564.3 1.0 fusion.82
  566.9 1.0 convolution_bitcast_fusion.6
  567.9 1.0 convolution_bitcast_fusion.7
  568.9 1.0 convolution_bitcast_fusion.8
  573.7 1.1 fusion.10
  574.8 2.9 convolution_convert_fusion
  (128 shorter events, 17.8 us)
Async XLA Ops:
  7.2 2.3 copy-start
  7.2 194.9 %reduce-scatter.2.cloned.1.call-start = ((), (), s32[]{:S(2)}) async-start(), calls=%async_computation.1 | async-start | bytes 3784704 | tf_op jit(solution)/shard_map/reduce_scatter | solution.py:71
  8.7 0.7 copy-start.27
  8.7 1.0 copy-start.30
  8.7 1.0 copy-start.31
  45.0 160.2 %copy-start.28 = (s32[2,128]{1,0:T(2,128)S(1)}, s32[2,128]{1,0:T(2,128)}, u32[]{:S(2)}) copy-start(s32[2,128]{1,0:T(2,128)} %constant.112.clone.1) | copy-start | bytes 3076
  45.0 286.1 %copy-start.26 = (f32[224]{0:T(256)S(1)}, f32[224]{0:T(256)}, u32[]{:S(2)}) copy-start(f32[224]{0:T(256)} %param.22) | copy-start | bytes 2692
  45.0 360.3 %copy-start.25 = (f32[2,256]{1,0:T(2,128)S(1)}, f32[2,256]{1,0:T(2,128)}, u32[]{:S(2)}) copy-start(f32[2,256]{1,0:T(2,128)} %param.23) | copy-start | bytes 6148
  45.0 360.3 %copy-start.29 = (f32[2]{0:T(128)S(1)}, f32[2]{0:T(128)}, u32[]{:S(2)}) copy-start(f32[2]{0:T(128)} %constant.126) | copy-start | bytes 28
  45.0 443.3 %copy-start.32 = (f32[2]{0:T(128)S(1)}, f32[2]{0:T(128)}, u32[]{:S(2)}) copy-start(f32[2]{0:T(128)} %constant.129) | copy-start | bytes 28
  45.0 449.5 %copy-start.22 = (f32[224,256]{1,0:T(8,128)S(1)}, f32[224,256]{1,0:T(8,128)}, u32[]{:S(2)}) copy-start(f32[224,256]{1,0:T(8,128)} %param.21) | copy-start | bytes 688132
  45.1 452.0 %copy-start.21 = (bf16[1,4,18,18,256]{4,1,3,2,0:T(4,128)(2,1)S(1)}, bf16[1,4,18,18,256]{4,1,3,2,0:T(4,128)(2,1)}, u32[]{:S(2)}) copy-start(bf16[1,4,18,18,256]{4,1,3,2,0:T(4,128)(2,1)} %param.24) | copy-start | bytes 1990660
  45.1 283.6 %all-gather.6.cloned.1.call-start = ((), (), s32[]{:S(2)}) async-start(), calls=%async_computation.3 | async-start | bytes 3899392 | tf_op jit(solution)/shard_map/all_gather | solution.py:76
  203.7 353.1 %all-gather.4.cloned.1.call-start = ((), (), s32[]{:S(2)}) async-start(), calls=%async_computation.2 | async-start | bytes 3784704 | tf_op jit(solution)/shard_map/all_gather | solution.py:101
  336.2 162.4 %copy-start.24 = (f32[224]{0:T(256)}, f32[224]{0:T(256)S(1)}, u32[]{:S(2)}) copy-start(f32[224]{0:T(256)S(1)} %get-tuple-element.32) | copy-start | bytes 2692
  405.4 93.2 %copy-start.23 = (f32[2,256]{1,0:T(2,128)}, f32[2,256]{1,0:T(2,128)S(1)}, u32[]{:S(2)}) copy-start(f32[2,256]{1,0:T(2,128)S(1)} %multiply_add_fusion) | copy-start | bytes 6148
  565.2 1.4 copy-start.4
  565.2 1.6 copy-start.3
  565.2 2.7 copy-start.2
  565.4 3.5 copy-start.1
  565.7 4.3 copy-start.20
  566.1 4.1 copy-start.19
  566.4 4.1 copy-start.18
  566.9 3.9 copy-start.17
  567.9 3.1 copy-start.16
  570.0 1.3 copy-start.14
  570.2 1.3 copy-start.12
  570.5 1.3 copy-start.15
  570.7 1.3 copy-start.13
  571.0 1.3 copy-start.11
  571.2 1.3 copy-start.10
  571.5 1.3 copy-start.9
  571.7 1.3 copy-start.8
  572.0 1.2 copy-start.7
  572.2 1.2 copy-start.6
  572.5 1.2 copy-start.5
Sparse Core Ops, SparseCore 0:
  45.2 156.8 reduce-scatter.1
  205.7 122.9 all-gather.5
  495.6 61.0 all-gather.3
